TPU v7x, 32 devices: a whole 2x2x4 slice. The times are simulated.
32 devices in a mesh: len: 8 (over z, y), wire: 4 (over x, core).
Axes of the slice: x: 2, y: 2, z: 4, core: 2. Of those that a mesh axis runs over, the one named last changes fastest.
Arguments:
- displacement: float32 [8, 4, 3, 3584], P('len', 'wire'), may hold values from -6 to 6
- previous: float32 [8, 4, 3, 3584], P('len', 'wire'), may hold values from -6 to 6
- element_nodes: int32 [8, 4, 125, 64], P('len', 'wire'), may hold values from 0 to 223
- element_stiffness: float32 [8, 4, 64], P('len', 'wire'), may hold values from 0.5 to 2
- gradient_op: float32 [375, 125], replicated, may hold values from -0.5 to 0.5
- mass_partial: float32 [8, 4, 3584], P('len', 'wire'), may hold values from 0.5 to 2
- left_ghost: int32 [8, 4, 768], P('len', 'wire'), may hold values from 0 to 3583, as said below
- right_ghost: int32 [8, 4, 768], P('len', 'wire'), may hold values from 0 to 3583, as said below
- contact_slots: int32 [8, 4, 4, 2048], P('len', 'wire'), may hold values from 0 to 3583
- contact_live: int32 [8, 4, 4, 2048], P('len', 'wire'), may hold values from 0 to 1, as said below
Outputs:
- final_field: float32 [8, 4, 3, 3584], P('len', 'wire')
- prior_field: float32 [8, 4, 3, 3584], P('len', 'wire')
Inputs may be any that keep to these rules, and one draw needn't show every extreme that they name: Within one piece the 768 slots of left_ghost and the 768 slots of right_ghost are all distinct. Within one piece the 768 slots of right_ghost and those of left_ghost are all distinct. contact_live[l, w, q, k] equals contact_live[l, q, w, k], and is 0 where q = w.
All inputs are finite; a program needn't handle non-finite values.
Results may differ from a plain program's by a relative error of at most 0.0003.
Values sent between devices are 32-bit elements; how exact they have to be, the bound alone decides.
A program may use at most 64 MiB of HBM per device.

v0:
```python
import functools

import jax
import jax.numpy as jnp
from jax import lax
from jax.experimental import pallas as pl
from jax.experimental.pallas import tpu as pltpu
from jax.sharding import PartitionSpec as P

ITERS = 4
PENALTY = 4.0
TIME_SQUARE = 0.03
block_slots = 224
block_elements = 4
LANES = 128
SUB = 8
f32 = jnp.float32
bf16 = jnp.bfloat16
MESH = pl.DeviceIdType.MESH


def round_up(value, step):
    return -(-value // step) * step


def dot(a, b):
    return jnp.dot(a, b, preferred_element_type=f32)


def dot_nt(a, b):
    return lax.dot_general(a, b, (((1,), (1,)), ((), ())), preferred_element_type=f32)


def block_kernel(grad_ref, nodes_ref, stiff_ref, out_ref, gram):
    node_count = grad_ref.shape[1]
    node_pad = gram.shape[0]
    wide = out_ref.shape[1]

    @pl.when(pl.program_id(0) == 0)
    def _():
        op = grad_ref[...]
        product = lax.dot_general(
            op, op, (((0,), (0,)), ((), ())), precision=lax.Precision.HIGHEST, preferred_element_type=f32
        )
        high = product.astype(bf16)
        gram[...] = jnp.zeros_like(gram)
        gram[:node_count, :node_count] = high
        gram[:node_count, node_pad : node_pad + node_count] = (product - high.astype(f32)).astype(bf16)

    nodes = nodes_ref[0]
    slot_ids = lax.broadcasted_iota(jnp.int32, (wide, nodes.shape[1]), 0)
    onehot = jnp.where(slot_ids == nodes, 1.0, 0.0).astype(bf16)
    pieces = []
    for e in range(block_elements):
        both = dot(onehot[:, e * node_pad : (e + 1) * node_pad], gram[...])
        pieces.append(both[:, :node_pad] + both[:, node_pad:])
    columns = jnp.concatenate(pieces, axis=1) * stiff_ref[0]
    high = columns.astype(bf16)
    low = (columns - high.astype(f32)).astype(bf16)
    operator = dot_nt(high, onehot) + dot_nt(low, onehot)
    high = operator.astype(bf16)
    out_ref[0, :, :wide] = high
    out_ref[0, :, wide:] = (operator - high.astype(f32)).astype(bf16)


def step_kernel(
    others,
    segments,
    chunk,
    u_in, p_in, mass_ref, op_ref, cb_ref, ci_ref, gb_ref, gi_ref,
    u_ref, p_ref,
    c_hot, g_hot, part, c_send, c_recv, g_send, g_recv,
    c_ssem, c_rsem, g_ssem, g_rsem,
):
    blocks = op_ref.shape[0]
    rows, wide = u_in.shape
    wires = others + 1
    pairs = cb_ref.shape[1] // others
    ghosts = gb_ref.shape[1] // 2
    me = lax.axis_index("wire")
    seg = lax.axis_index("len")
    has_prev = seg > 0
    has_next = seg < segments - 1

    def partner(d):
        return lax.rem(me + (d + 1), wires)

    barrier = pltpu.get_barrier_semaphore()
    for d in range(others):
        pl.semaphore_signal(barrier, inc=1, device_id={"wire": partner(d)}, device_id_type=MESH)

    @pl.when(has_prev)
    def _():
        pl.semaphore_signal(barrier, inc=1, device_id={"len": seg - 1}, device_id_type=MESH)

    @pl.when(has_next)
    def _():
        pl.semaphore_signal(barrier, inc=1, device_id={"len": seg + 1}, device_id_type=MESH)

    def fill(hot, index_ref):
        count = index_ref.shape[1]
        step = 512 if count % 512 == 0 else LANES

        def body(i, _):
            cols = pl.ds(pl.multiple_of(i * step, step), step)
            ids = lax.broadcasted_iota(jnp.int32, (wide, step), 0)
            hot[:, cols] = jnp.where(ids == index_ref[:, cols], 1.0, 0.0).astype(bf16)
            return 0

        lax.fori_loop(0, count // step, body, 0)

    fill(c_hot, ci_ref)
    fill(g_hot, gi_ref)
    u_ref[...] = u_in[...]
    p_ref[...] = p_in[...]

    @pl.when(jnp.logical_not(has_prev))
    def _():
        g_recv[:, 0] = jnp.zeros((ITERS,) + g_recv.shape[2:], f32)

    @pl.when(jnp.logical_not(has_next))
    def _():
        g_recv[:, 1] = jnp.zeros((ITERS,) + g_recv.shape[2:], f32)

    last = segments - 1
    pl.semaphore_wait(
        barrier, others + lax.div(seg + last, segments) + lax.div(last - seg + last, segments)
    )

    row_all = lax.broadcasted_iota(jnp.int32, (rows, wide), 0) & (SUB - 1)
    low_all = row_all < 4

    def rows_of(width):
        return lax.broadcasted_iota(jnp.int32, (SUB, width), 0)

    def split(x):
        high = x.astype(bf16).astype(f32)
        return jnp.where(low_all, high, pltpu.roll(x - high, 4, 0)).astype(bf16)

    def take(packed, hot, base_ref, start, width):
        cols = slice(start, start + width)
        picked = dot(packed, hot[:, cols])
        which = jnp.broadcast_to(base_ref[:, cols], (SUB, width))
        total = jnp.zeros((SUB, width), f32)
        for b in range(blocks):
            total = jnp.where(which == b, picked[b * SUB : (b + 1) * SUB], total)
        return total + pltpu.roll(total, 4, 0)

    def put(values, hot, base_ref, start, width):
        cols = slice(start, start + width)
        high = values.astype(bf16).astype(f32)
        values = jnp.where(rows_of(width) < 4, high, values - high)
        which = jnp.broadcast_to(base_ref[:, cols], (SUB, width))
        spread = jnp.concatenate([jnp.where(which == b, values, 0.0) for b in range(blocks)], axis=0)
        return dot_nt(spread.astype(bf16), hot[:, cols])

    def take_list(packed, hot, base_ref, start, count, out_ref):
        half = count // 2
        width = chunk if half % chunk == 0 else half
        for at in range(0, half, width):
            first = take(packed, hot, base_ref, start + at, width)
            second = take(packed, hot, base_ref, start + half + at, width)
            out_ref[:, at : at + width] = jnp.where(rows_of(width) < 4, first, second)

    def put_list(values, hot, base_ref, start, count, total):
        half = count // 2
        width = chunk if half % chunk == 0 else half
        for at in range(0, half, width):
            here = values[:, at : at + width]
            turned = pltpu.roll(here, 4, 0)
            low = rows_of(width) < 4
            total = total + put(jnp.where(low, here, turned), hot, base_ref, start + at, width)
            total = total + put(jnp.where(low, turned, here), hot, base_ref, start + half + at, width)
        return total

    def contact_copy(step, d):
        return pltpu.make_async_remote_copy(
            src_ref=c_send.at[d],
            dst_ref=c_recv.at[step, others - 1 - d],
            send_sem=c_ssem.at[d],
            recv_sem=c_rsem.at[step, others - 1 - d],
            device_id={"wire": partner(d)},
            device_id_type=MESH,
        )

    def contact_arrival(step, d):
        return pltpu.make_async_remote_copy(
            src_ref=c_send.at[d],
            dst_ref=c_recv.at[step, d],
            send_sem=c_ssem.at[d],
            recv_sem=c_rsem.at[step, d],
            device_id={"wire": partner(d)},
            device_id_type=MESH,
        )

    def ghost_copy(step, side):
        return pltpu.make_async_remote_copy(
            src_ref=g_send.at[side],
            dst_ref=g_recv.at[step, 1 - side],
            send_sem=g_ssem.at[side],
            recv_sem=g_rsem.at[step, 1 - side],
            device_id={"len": seg - 1 if side == 0 else seg + 1},
            device_id_type=MESH,
        )

    def ghost_arrival(step, side):
        return pltpu.make_async_remote_copy(
            src_ref=g_send.at[side],
            dst_ref=g_recv.at[step, side],
            send_sem=g_ssem.at[side],
            recv_sem=g_rsem.at[step, side],
            device_id={"len": seg - 1 if side == 0 else seg + 1},
            device_id_type=MESH,
        )

    exists = (has_prev, has_next)

    def one_step(step, _):
        packed = split(u_ref[...])
        for d in range(others):
            take_list(packed, c_hot, cb_ref, d * pairs, pairs, c_send.at[d])
            contact_copy(step, d).start()

        for b in range(blocks):
            pair = packed[(b // 2) * 2 * SUB : (b // 2 + 1) * 2 * SUB]
            out = dot(pair, op_ref[b])[(b % 2) * SUB : (b % 2 + 1) * SUB]
            main = out[:, :wide]
            part[b * SUB : (b + 1) * SUB, :] = main + pltpu.roll(main, 4, 0) + out[:, wide:]

        spread = jnp.zeros((rows, wide), f32)
        for d in range(others):
            contact_arrival(step, d).wait_recv()
            spread = put_list(c_recv[step, d] - c_send[d], c_hot, cb_ref, d * pairs, pairs, spread)
        spread = spread + pltpu.roll(spread, rows - 4, 0)
        local = jnp.where(row_all < 3, PENALTY * spread - part[...], mass_ref[...])
        part[...] = local

        packed = split(local)
        for side in range(2):
            take_list(packed, g_hot, gb_ref, side * ghosts, ghosts, g_send.at[side])

            @pl.when(exists[side])
            def _():
                ghost_copy(step, side).start()

        spread = jnp.zeros((rows, wide), f32)
        for side in range(2):

            @pl.when(exists[side])
            def _():
                ghost_arrival(step, side).wait_recv()

            spread = put_list(g_recv[step, side], g_hot, gb_ref, side * ghosts, ghosts, spread)
        spread = spread + pltpu.roll(spread, rows - 4, 0)
        total = jnp.where(low_all, part[...] + spread, 0.0)
        for b in range(blocks):
            at = slice(b * SUB, (b + 1) * SUB)
            force = total[at]
            mass = jnp.broadcast_to(force[3:4], force.shape)
            now = u_ref[at, :]
            stepped = 2.0 * now - p_ref[at, :] + TIME_SQUARE * force / mass
            p_ref[at, :] = now
            u_ref[at, :] = jnp.where(rows_of(wide) < 3, stepped, 0.0)

        for d in range(others):
            contact_copy(step, d).wait_send()
        for side in range(2):

            @pl.when(exists[side])
            def _():
                ghost_copy(step, side).wait_send()

        return 0

    lax.fori_loop(0, ITERS, one_step, 0)


def on_device(
    displacement, previous, element_nodes, element_stiffness, gradient_op,
    mass_partial, left_ghost, right_ghost, contact_slots, contact_live,
):
    nodes = element_nodes[0, 0]
    node_count, elements = nodes.shape
    blocks = elements // block_elements
    wide = round_up(block_slots, 2 * LANES)
    node_pad = round_up(node_count, LANES)
    segments = lax.axis_size("len")
    wires = lax.axis_size("wire")
    others = wires - 1
    me = lax.axis_index("wire")
    slots = displacement.shape[3]
    parts = displacement.shape[2]
    rows = blocks * SUB

    nodes_t = jnp.pad(nodes.T, ((0, 0), (0, node_pad - node_count)), constant_values=-1)
    nodes_t = nodes_t.reshape(blocks, 1, block_elements * node_pad)
    stiff = jnp.repeat(element_stiffness[0, 0], node_pad).reshape(blocks, 1, block_elements * node_pad)

    vmem = pl.BlockSpec(memory_space=pltpu.VMEM)
    operators = pl.pallas_call(
        block_kernel,
        grid=(blocks,),
        out_shape=jax.ShapeDtypeStruct((blocks, wide, 2 * wide), bf16),
        in_specs=[
            pl.BlockSpec(gradient_op.shape, lambda b: (0, 0)),
            pl.BlockSpec((1, 1, block_elements * node_pad), lambda b: (b, 0, 0)),
            pl.BlockSpec((1, 1, block_elements * node_pad), lambda b: (b, 0, 0)),
        ],
        out_specs=pl.BlockSpec((1, wide, 2 * wide), lambda b: (b, 0, 0)),
        scratch_shapes=[pltpu.VMEM((node_pad, 2 * node_pad), bf16)],
        name="operators",
    )(gradient_op, nodes_t, stiff)

    def lay(field, row):
        count = field.shape[0]
        field = field.reshape(count, blocks, block_slots).transpose(1, 0, 2)
        return jnp.pad(field, ((0, 0), (row, SUB - row - count), (0, wide - block_slots)))

    u = lay(displacement[0, 0], 0).reshape(rows, wide)
    p = lay(previous[0, 0], 0).reshape(rows, wide)
    mass = mass_partial[0, 0].reshape(blocks, 1, block_slots)
    mass = jnp.pad(mass, ((0, 0), (0, 0), (0, wide - block_slots)), constant_values=1.0)
    mass = jnp.pad(mass, ((0, 0), (3, SUB - 4), (0, 0))).reshape(rows, wide)

    def from_me(x):
        return lax.dynamic_slice_in_dim(jnp.concatenate([x, x], axis=0), me + 1, others, axis=0)

    pair_slots = from_me(contact_slots[0, 0]).reshape(1, -1)
    live = from_me(contact_live[0, 0]).reshape(1, -1)
    c_block = jnp.where(live > 0, pair_slots // block_slots, -1)
    c_index = pair_slots % block_slots
    ghost = jnp.concatenate([left_ghost[0, 0], right_ghost[0, 0]])[None]
    pairs = contact_slots.shape[3]
    ghosts = left_ghost.shape[2]

    u, p = pl.pallas_call(
        functools.partial(step_kernel, others, segments, 512),
        out_shape=[jax.ShapeDtypeStruct((rows, wide), f32)] * 2,
        in_specs=[vmem] * 8,
        out_specs=[vmem] * 2,
        scratch_shapes=[
            pltpu.VMEM((wide, others * pairs), bf16),
            pltpu.VMEM((wide, 2 * ghosts), bf16),
            pltpu.VMEM((rows, wide), f32),
            pltpu.VMEM((others, SUB, pairs // 2), f32),
            pltpu.VMEM((ITERS, others, SUB, pairs // 2), f32),
            pltpu.VMEM((2, SUB, ghosts // 2), f32),
            pltpu.VMEM((ITERS, 2, SUB, ghosts // 2), f32),
            pltpu.SemaphoreType.DMA((others,)),
            pltpu.SemaphoreType.DMA((ITERS, others)),
            pltpu.SemaphoreType.DMA((2,)),
            pltpu.SemaphoreType.DMA((ITERS, 2)),
        ],
        compiler_params=pltpu.CompilerParams(
            collective_id=0, has_side_effects=True, vmem_limit_bytes=48 * 1024 * 1024
        ),
        name="steps",
    )(u, p, mass, operators, c_block, c_index, ghost // block_slots, ghost % block_slots)

    def unlay(x):
        x = x.reshape(blocks, SUB, wide)[:, :parts, :block_slots]
        return x.transpose(1, 0, 2).reshape(1, 1, parts, slots)

    return unlay(u), unlay(p)


def solution(mesh):
    four = P("len", "wire", None, None)
    three = P("len", "wire", None)
    return jax.shard_map(
        on_device,
        mesh=mesh,
        in_specs=(four, four, four, three, P(), three, three, three, four, four),
        out_specs=(four, four),
        check_vma=False,
    )
```

profile of v0, /device:TPU:0, one launch (start us, length us, event | category | flops | bytes accessed | tf_op | source)
XLA Modules:
  0.0 65.9 jit_solution(740498830575420957)
XLA Ops:
  0.6 0.5 broadcast.195
  1.1 1.3 %reduce.6 = f32[64]{0:T(128)S(1)} reduce(f32[1,1,64]{2,1,0:T(1,128)} %param.13, f32[]{:T(128)} %broadcast.195), dimensions={0,1}, to_apply=%param.13.reduce_sub_computation.3 | reduce | bytes 516 | tf_op args[3]
  2.5 0.1 broadcast_in_dim.10
  2.5 0.9 %fusion.5 = pred[1,1,3,2048]{3,2,1,0:T(4,128)(4,1)S(1)} fusion(s32[]{:T(128)S(6)} %select_n.39, s32[4,2048]{1,0:T(4,128)} %bitcast.54), kind=kLoop, calls=%fused_computation.23 | loop fusion | flops 12288 | bytes 38916
  3.4 0.8 %and_select_fusion.2 = (s32[1,1536]{1,0:T(1,128)S(1)}, s32[1,1536]{1,0:T(1,128)S(1)}) fusion(s32[1,768]{1,0:T(1,128)} %bitcast.56, s32[1,768]{1,0:T(1,128)} %bitcast.57), kind=kLoop, calls=%fused_computation.25 | loop fusion | flops 19968 | bytes 18432 | tf_op jit(solution)/shard_map/jit(remainder)/select_n | solution.py:358
  4.2 0.8 %reduce.2 = f32[3584]{0:T(1024)S(1)} reduce(f32[1,1,3584]{2,1,0:T(1,128)} %param.15, f32[]{:T(128)} %constant.65), dimensions={0,1}, to_apply=%param.15.reduce_sub_computation | reduce | bytes 28676 | tf_op args[5]
  5.0 0.1 reshape_squeeze.12
  5.1 0.7 %broadcast_in_dim.11 = f32[16,4,128]{2,1,0:T(4,128)} broadcast(f32[16,4]{1,0:T(8,128)S(1)} %broadcast_in_dim.10), dimensions={0,1} | broadcast | bytes 33024 | tf_op jit(solution)/shard_map/broadcast_in_dim | solution.py:297
  5.8 1.4 %pad.23 = s32[64,128]{1,0:T(8,128)} pad(s32[64,125]{1,0:T(8,128)} %bitcast.55, s32[]{:T(128)} %constant.40.clone.1), padding=0_0x0_3 | pad | bytes 64772 | tf_op jit(solution)/shard_map/jit(_pad)/pad | solution.py:295
  7.2 0.9 %reduce = f32[3,3584]{1,0:T(4,128)S(1)} reduce(f32[1,1,3,3584]{3,1,2,0:T(1,128)} %param.10, f32[]{:T(128)} %constant.65), dimensions={0,1}, to_apply=%param.10.reduce_sub_computation | reduce | bytes 86020 | tf_op args[0]
  8.1 0.1 reshape_squeeze.9
  8.2 0.9 %reduce.1 = f32[3,3584]{1,0:T(4,128)S(1)} reduce(f32[1,1,3,3584]{3,1,2,0:T(1,128)} %param.11, f32[]{:T(128)} %constant.65), dimensions={0,1}, to_apply=%param.11.reduce_sub_computation | reduce | bytes 86020 | tf_op args[1]
  9.1 0.1 reshape_squeeze.10
  9.3 0.9 %remainder_bitcast_fusion = (s32[1,1,3,2048]{3,2,1,0:T(4,128)S(1)}, s32[3,2048]{1,0:T(4,128)S(1)}) fusion(s32[]{:T(128)S(6)} %select_n.39, s32[4,2048]{1,0:T(4,128)} %bitcast.53), kind=kLoop, calls=%fused_computation.20 | loop fusion | flops 12288 | bytes 81924
  10.3 0.1 and_select_fusion
  10.5 13.1 %operators.1.op_ref = bf16[16,256,512]{2,1,0:T(8,128)(2,1)} custom-call(f32[375,125]{1,0:T(8,128)} %grad_ref.1, s32[16,1,512]{2,1,0:T(1,128)} %bitcast.48, f32[16,1,512]{2,1,0:T(1,128)} %bitcast.47), custom_call_target="tpu_custom_call" | custom-call | tf_op jit(solution)/shard_map/operators/pallas_call | solution.py:300
  23.6 0.0 copy-start
  23.6 2.2 %copy-done = bf16[16,256,512]{2,1,0:T(8,128)(2,1)S(1)} copy-done((bf16[16,256,512]{2,1,0:T(8,128)(2,1)S(1)}, bf16[16,256,512]{2,1,0:T(8,128)(2,1)}, u32[]{:S(2)}) %copy-start) | copy-done | bytes 4194328
  25.8 38.6 %steps.1 = (f32[128,256]{1,0:T(8,128)S(1)}, f32[128,256]{1,0:T(8,128)S(1)}) custom-call(f32[128,256]{1,0:T(8,128)S(1)} %pad_bitcast_fusion.1.u_in, f32[128,256]{1,0:T(8,128)S(1)} %get-tuple-element.13.p_in, f32[128,256]{1,0:T(8,128)S(1)} %get-tuple-element.12.mass_ref, bf16[16,256,512]{2,1,0:T(8,128)(2,1)S(1)} %copy-done, ...), custom_call_target="tpu_custom_call" | custom-call | tf_op jit(solution)/shard_map/steps/pallas_call | solution.py:336
  64.4 0.7 %reshape.289 = f32[1,1,3,3584]{3,1,2,0:T(1,128)} reshape(f32[3,16,224]{2,1,0:T(8,128)S(1)} %copy.20) | data formatting | bytes 86016 | tf_op jit(solution)/shard_map/reshape | solution.py:362
  65.2 0.7 %reshape.291 = f32[1,1,3,3584]{3,1,2,0:T(1,128)} reshape(f32[3,16,224]{2,1,0:T(8,128)S(1)} %copy.21) | data formatting | bytes 86016 | tf_op jit(solution)/shard_map/reshape | solution.py:362
  (14 shorter events, 0.3 us)
Async XLA Ops:
  23.6 2.2 %copy-start = (bf16[16,256,512]{2,1,0:T(8,128)(2,1)S(1)}, bf16[16,256,512]{2,1,0:T(8,128)(2,1)}, u32[]{:S(2)}) copy-start(bf16[16,256,512]{2,1,0:T(8,128)(2,1)} %operators.1.op_ref) | copy-start | bytes 12582916
where the time goes:
time: 66.9 us; the launch traced here: 65.9 us
  Pallas kernels  51.6 us (77%)
  local copies, waits for them, and re-layouts  6.86 us (10%)
  other arithmetic  6.63 us (10%)
  between operations  0.78 us (1%)
    pallas_call x1, Pallas kernels, on_device(): pl.pallas_call(functools.partial(step_kernel, others, segments, 512), out...  38.6 us
    pallas_call x1, Pallas kernels, on_device(): pl.pallas_call(block_kernel, grid=(blocks,), out_shape=jax.ShapeDtypeStru...  13.1 us
    unnamed x8, other arithmetic  5.72 us
    unnamed x7, local copies, waits for them, and re-layouts  2.81 us
    reshape x2, local copies, waits for them, and re-layouts, unlay(): return x.transpose(1, 0, 2).reshape(1, 1, parts, slots)  1.47 us
    pad x1, local copies, waits for them, and re-layouts, on_device(): jnp.pad(nodes.T, ((0, 0), (0, node_pad - node_count)), constant_values=-1)  1.38 us

commit v1 on v0

v1 whole, which is shorter than its diff:
```python
import functools

import jax
import jax.numpy as jnp
from jax import lax
from jax.experimental import pallas as pl
from jax.experimental.pallas import tpu as pltpu
from jax.sharding import PartitionSpec as P

ITERS = 4
PENALTY = 4.0
TIME_SQUARE = 0.03
block_slots = 224
block_elements = 4
LANES = 128
BLOCK_SCALE, BLOCK_SHIFT = 4682, 20
SUB = 8
f32 = jnp.float32
bf16 = jnp.bfloat16
MESH = pl.DeviceIdType.MESH


def round_up(value, step):
    return -(-value // step) * step


def dot(a, b):
    return jnp.dot(a, b, preferred_element_type=f32)


def dot_nt(a, b):
    return lax.dot_general(a, b, (((1,), (1,)), ((), ())), preferred_element_type=f32)


def step_kernel(
    wires,
    segments,
    chunk,
    u_in, p_in, nodes_in, stiff_in, grad_in, mass_in, left_in, right_in, slots_in, live_in,
    u_out, p_out,
    u_ref, p_ref, mass_ref,
    c_hot, g_hot, e_hot, cb_ref, gb_ref, gram, nodes_ref, stiff_ref,
    part, picked, c_send, c_recv, g_send, g_recv,
    c_ssem, c_rsem, g_ssem, g_rsem,
):
    others = wires - 1
    blocks = e_hot.shape[0]
    parts = u_in.shape[1]
    rows, wide = u_ref.shape
    pairs = slots_in.shape[3]
    ghosts = left_in.shape[2]
    elements, node_count = nodes_in.shape[2:]
    node_pad = gram.shape[0]
    me = lax.axis_index("wire")
    seg = lax.axis_index("len")
    has_prev = seg > 0
    has_next = seg < segments - 1
    mirrored = wires & (wires - 1) == 0

    def partner(d):
        if not mirrored:
            return lax.rem(me + (d + 1), wires)
        offset, other, bit = wires - 1 - d, me, 1
        while bit <= offset:
            if offset & bit:
                other = other + bit - 2 * bit * lax.rem(lax.div(me, bit), 2)
            bit *= 2
        return other

    def landing(d):
        return d if mirrored else others - 1 - d

    barrier = pltpu.get_barrier_semaphore()
    for d in range(others):
        pl.semaphore_signal(barrier, inc=1, device_id={"wire": partner(d)}, device_id_type=MESH)

    @pl.when(has_prev)
    def _():
        pl.semaphore_signal(barrier, inc=1, device_id={"len": seg - 1}, device_id_type=MESH)

    @pl.when(has_next)
    def _():
        pl.semaphore_signal(barrier, inc=1, device_id={"len": seg + 1}, device_id_type=MESH)

    def block_of(slots):
        return (slots * BLOCK_SCALE) >> BLOCK_SHIFT

    def fill(hot, base_ref, at, slots, live):
        count = slots.shape[1]
        which = block_of(slots)
        inside = slots - which * block_slots
        if live is not None:
            which = jnp.where(live > 0, which, -1)
        base_ref[:, at : at + count] = jnp.broadcast_to(which, (SUB, count))
        for start in range(0, count, LANES):
            ids = lax.broadcasted_iota(jnp.int32, (wide, LANES), 0)
            here = inside[:, start : start + LANES]
            hot[:, at + start : at + start + LANES] = jnp.where(ids == here, 1.0, 0.0).astype(bf16)

    u_ref[...] = jnp.zeros_like(u_ref)
    p_ref[...] = jnp.zeros_like(p_ref)
    for b in range(blocks):
        lanes = slice(b * block_slots, (b + 1) * block_slots)
        for c in range(parts):
            row = slice(b * SUB + c, b * SUB + c + 1)
            u_ref[row, :block_slots] = u_in[0, c, :, lanes]
            p_ref[row, :block_slots] = p_in[0, c, :, lanes]
    for d in range(others):
        fill(c_hot, cb_ref, d * pairs, slots_in[0, 0, pl.ds(partner(d), 1), :], live_in[0, 0, pl.ds(partner(d), 1), :])

    @pl.when(jnp.logical_not(has_prev))
    def _():
        g_recv[:, 0] = jnp.zeros((ITERS,) + g_recv.shape[2:], f32)

    @pl.when(jnp.logical_not(has_next))
    def _():
        g_recv[:, 1] = jnp.zeros((ITERS,) + g_recv.shape[2:], f32)

    def prepare():
        row8 = lax.broadcasted_iota(jnp.int32, (SUB, wide), 0)
        lane8 = lax.broadcasted_iota(jnp.int32, (SUB, wide), 1)
        for b in range(blocks):
            at = slice(b * SUB, (b + 1) * SUB)
            lanes = slice(b * block_slots, (b + 1) * block_slots)
            mass_ref[at, :] = jnp.where((row8 == 3) & (lane8 >= block_slots), 1.0, 0.0)
            mass_ref[b * SUB + 3 : b * SUB + 4, :block_slots] = mass_in[0, :, lanes]
        fill(g_hot, gb_ref, 0, left_in[0], None)
        fill(g_hot, gb_ref, ghosts, right_in[0], None)
        op = grad_in[...]
        product = lax.dot_general(
            op, op, (((0,), (0,)), ((), ())), precision=lax.Precision.HIGHEST, preferred_element_type=f32
        )
        high = product.astype(bf16)
        gram[...] = jnp.zeros_like(gram)
        gram[:node_count, :node_count] = high
        gram[:node_count, node_pad : node_pad + node_count] = (product - high.astype(f32)).astype(bf16)
        nodes_ref[...] = jnp.full(nodes_ref.shape, -1, jnp.int32)
        nodes_ref[:, :node_count] = nodes_in[0, 0]
        stiff_ref[...] = jnp.zeros_like(stiff_ref)
        stiff_ref[:, :elements] = jnp.broadcast_to(stiff_in[0], (stiff_ref.shape[0], elements))
        stiff_ref[...] = jnp.transpose(stiff_ref[...])
        for b in range(blocks):
            for e in range(block_elements):
                one = b * block_elements + e
                ids = lax.broadcasted_iota(jnp.int32, (wide, node_pad), 0)
                hot = jnp.where(ids == nodes_ref[one : one + 1, :], 1.0, 0.0).astype(bf16)
                e_hot[b, :, e * node_pad : (e + 1) * node_pad] = hot

    last = segments - 1
    pl.semaphore_wait(
        barrier, others + lax.div(seg + last, segments) + lax.div(last - seg + last, segments)
    )

    row_all = lax.broadcasted_iota(jnp.int32, (rows, wide), 0) & (SUB - 1)
    low_all = row_all < 4

    def rows_of(width):
        return lax.broadcasted_iota(jnp.int32, (SUB, width), 0)

    def split(x):
        high = x.astype(bf16).astype(f32)
        return jnp.where(low_all, high, pltpu.roll(x - high, 4, 0)).astype(bf16)

    def take(packed, hot, base_ref, start, width):
        cols = slice(start, start + width)
        picked = dot(packed, hot[:, cols])
        which = base_ref[:, cols]
        total = jnp.zeros((SUB, width), f32)
        for b in range(blocks):
            total = jnp.where(which == b, picked[b * SUB : (b + 1) * SUB], total)
        return total + pltpu.roll(total, 4, 0)

    def put(values, hot, base_ref, start, width):
        cols = slice(start, start + width)
        high = values.astype(bf16).astype(f32)
        values = jnp.where(rows_of(width) < 4, high, values - high)
        which = base_ref[:, cols]
        spread = jnp.concatenate([jnp.where(which == b, values, 0.0) for b in range(blocks)], axis=0)
        return dot_nt(spread.astype(bf16), hot[:, cols])

    def take_list(packed, hot, base_ref, start, count, out_ref):
        half = count // 2
        width = chunk if half % chunk == 0 else half
        for at in range(0, half, width):
            first = take(packed, hot, base_ref, start + at, width)
            second = take(packed, hot, base_ref, start + half + at, width)
            out_ref[:, at : at + width] = jnp.where(rows_of(width) < 4, first, second)

    def put_list(values, hot, base_ref, start, count, total):
        half = count // 2
        width = chunk if half % chunk == 0 else half
        for at in range(0, half, width):
            here = values[:, at : at + width]
            turned = pltpu.roll(here, 4, 0)
            low = rows_of(width) < 4
            total = total + put(jnp.where(low, here, turned), hot, base_ref, start + at, width)
            total = total + put(jnp.where(low, turned, here), hot, base_ref, start + half + at, width)
        return total

    def contact_copy(step, d):
        return pltpu.make_async_remote_copy(
            src_ref=c_send.at[d],
            dst_ref=c_recv.at[step, landing(d)],
            send_sem=c_ssem.at[d],
            recv_sem=c_rsem.at[step, landing(d)],
            device_id={"wire": partner(d)},
            device_id_type=MESH,
        )

    def contact_arrival(step, d):
        return pltpu.make_async_remote_copy(
            src_ref=c_send.at[d],
            dst_ref=c_recv.at[step, d],
            send_sem=c_ssem.at[d],
            recv_sem=c_rsem.at[step, d],
            device_id={"wire": partner(d)},
            device_id_type=MESH,
        )

    def ghost_copy(step, side):
        return pltpu.make_async_remote_copy(
            src_ref=g_send.at[side],
            dst_ref=g_recv.at[step, 1 - side],
            send_sem=g_ssem.at[side],
            recv_sem=g_rsem.at[step, 1 - side],
            device_id={"len": seg - 1 if side == 0 else seg + 1},
            device_id_type=MESH,
        )

    def ghost_arrival(step, side):
        return pltpu.make_async_remote_copy(
            src_ref=g_send.at[side],
            dst_ref=g_recv.at[step, side],
            send_sem=g_ssem.at[side],
            recv_sem=g_rsem.at[step, side],
            device_id={"len": seg - 1 if side == 0 else seg + 1},
            device_id_type=MESH,
        )

    exists = (has_prev, has_next)

    def one_step(step, _):
        packed = split(u_ref[...])
        for d in range(others):
            take_list(packed, c_hot, cb_ref, d * pairs, pairs, c_send.at[d])
            contact_copy(step, d).start()

        @pl.when(step == 0)
        def _():
            prepare()

        both = 2 * SUB
        for b in range(blocks):
            pair = packed[(b // 2) * both : (b // 2 + 1) * both]
            out = dot(pair, e_hot[b])[(b % 2) * SUB : (b % 2 + 1) * SUB]
            for e in range(block_elements):
                one = b * block_elements + e
                picked[one * SUB : (one + 1) * SUB, :] = out[:, e * node_pad : (e + 1) * node_pad]
        reach = elements * SUB // 4
        for at in range(0, elements * SUB, reach):
            out = dot(picked[at : at + reach, :].astype(bf16), gram[...])
            main = out[:, :node_pad]
            main = main + pltpu.roll(main, reach - 4, 0) + out[:, node_pad:]
            for i in range(0, reach, SUB):
                one = (at + i) // SUB
                r = main[i : i + SUB] * jnp.broadcast_to(stiff_ref[one : one + 1, :], (SUB, node_pad))
                high = r.astype(bf16).astype(f32)
                low = jnp.where(rows_of(node_pad) < 4, high, pltpu.roll(r - high, 4, 0))
                picked[at + i : at + i + SUB, :] = low
        for b in range(0, blocks, 2):
            pair = jnp.concatenate(
                [
                    jnp.concatenate(
                        [
                            picked[one * SUB : (one + 1) * SUB, :]
                            for one in range(k * block_elements, (k + 1) * block_elements)
                        ],
                        axis=1,
                    )
                    for k in (b, b + 1)
                ],
                axis=0,
            ).astype(bf16)
            for k in range(2):
                out = dot_nt(pair, e_hot[b + k])[k * SUB : (k + 1) * SUB]
                part[(b + k) * SUB : (b + k + 1) * SUB, :] = out + pltpu.roll(out, 4, 0)

        spread = jnp.zeros((rows, wide), f32)
        for d in reversed(range(others)):
            contact_arrival(step, d).wait_recv()
            spread = put_list(c_recv[step, d] - c_send[d], c_hot, cb_ref, d * pairs, pairs, spread)
        spread = spread + pltpu.roll(spread, rows - 4, 0)
        local = jnp.where(row_all < 3, PENALTY * spread - part[...], mass_ref[...])
        part[...] = local

        packed = split(local)
        for side in range(2):
            take_list(packed, g_hot, gb_ref, side * ghosts, ghosts, g_send.at[side])

            @pl.when(exists[side])
            def _():
                ghost_copy(step, side).start()

        spread = jnp.zeros((rows, wide), f32)
        for side in range(2):

            @pl.when(exists[side])
            def _():
                ghost_arrival(step, side).wait_recv()

            spread = put_list(g_recv[step, side], g_hot, gb_ref, side * ghosts, ghosts, spread)
        spread = spread + pltpu.roll(spread, rows - 4, 0)
        total = jnp.where(low_all, part[...] + spread, 0.0)
        for b in range(blocks):
            at = slice(b * SUB, (b + 1) * SUB)
            force = total[at]
            mass = jnp.broadcast_to(force[3:4], force.shape)
            now = u_ref[at, :]
            stepped = 2.0 * now - p_ref[at, :] + TIME_SQUARE * force / mass
            p_ref[at, :] = now
            u_ref[at, :] = jnp.where(rows_of(wide) < 3, stepped, 0.0)

        for d in range(others):
            contact_copy(step, d).wait_send()
        for side in range(2):

            @pl.when(exists[side])
            def _():
                ghost_copy(step, side).wait_send()

        return 0

    lax.fori_loop(0, ITERS, one_step, 0)
    for b in range(blocks):
        lanes = slice(b * block_slots, (b + 1) * block_slots)
        for c in range(parts):
            row = slice(b * SUB + c, b * SUB + c + 1)
            u_out[0, c, :, lanes] = u_ref[row, :block_slots]
            p_out[0, c, :, lanes] = p_ref[row, :block_slots]


def on_device(displacement, previous, element_nodes, *rest):
    left_ghost, contact_slots = rest[3], rest[5]
    node_count, elements = element_nodes.shape[2:]
    blocks = elements // block_elements
    wide = round_up(block_slots, 2 * LANES)
    node_pad = round_up(node_count, LANES)
    wires = lax.axis_size("wire")
    others = wires - 1
    rows = blocks * SUB
    pairs = contact_slots.shape[3]
    ghosts = left_ghost.shape[2]
    assert blocks % 2 == 0 and elements <= LANES and node_pad == LANES
    assert all((x * BLOCK_SCALE) >> BLOCK_SHIFT == x // block_slots for x in range(blocks * block_slots))

    vmem = pl.BlockSpec(memory_space=pltpu.VMEM)
    turned = jnp.swapaxes(displacement, 1, 2)
    args = (turned, jnp.swapaxes(previous, 1, 2), jnp.swapaxes(element_nodes, 2, 3), *rest)
    results = pl.pallas_call(
        functools.partial(step_kernel, wires, lax.axis_size("len"), 512),
        out_shape=[jax.ShapeDtypeStruct(turned.shape, f32)] * 2,
        in_specs=[vmem] * len(args),
        out_specs=[vmem] * 2,
        scratch_shapes=[
            pltpu.VMEM((rows, wide), f32),
            pltpu.VMEM((rows, wide), f32),
            pltpu.VMEM((rows, wide), f32),
            pltpu.VMEM((wide, others * pairs), bf16),
            pltpu.VMEM((wide, 2 * ghosts), bf16),
            pltpu.VMEM((blocks, wide, block_elements * node_pad), bf16),
            pltpu.VMEM((SUB, others * pairs), jnp.int32),
            pltpu.VMEM((SUB, 2 * ghosts), jnp.int32),
            pltpu.VMEM((node_pad, 2 * node_pad), bf16),
            pltpu.VMEM((elements, node_pad), jnp.int32),
            pltpu.VMEM((LANES, LANES), f32),
            pltpu.VMEM((rows, wide), f32),
            pltpu.VMEM((elements * SUB, node_pad), f32),
            pltpu.VMEM((others, SUB, pairs // 2), f32),
            pltpu.VMEM((ITERS, others, SUB, pairs // 2), f32),
            pltpu.VMEM((2, SUB, ghosts // 2), f32),
            pltpu.VMEM((ITERS, 2, SUB, ghosts // 2), f32),
            pltpu.SemaphoreType.DMA((others,)),
            pltpu.SemaphoreType.DMA((ITERS, others)),
            pltpu.SemaphoreType.DMA((2,)),
            pltpu.SemaphoreType.DMA((ITERS, 2)),
        ],
        compiler_params=pltpu.CompilerParams(
            collective_id=0, has_side_effects=True, vmem_limit_bytes=48 * 1024 * 1024
        ),
        name="steps",
    )(*args)
    return tuple(jnp.swapaxes(x, 1, 2) for x in results)


def solution(mesh):
    four = P("len", "wire", None, None)
    three = P("len", "wire", None)
    return jax.shard_map(
        on_device,
        mesh=mesh,
        in_specs=(four, four, four, three, P(), three, three, three, four, four),
        out_specs=(four, four),
        check_vma=False,
    )
```

time: 66.9 us -> 51.7 us (0.77)
  Pallas kernels: 51.6 us -> 42.4 us
  other arithmetic: 6.63 us -> 0 us
  local copies, waits for them, and re-layouts: 6.86 us -> 8.07 us
    pallas_call x2 -> x1, Pallas kernels: 51.6 us -> 42.4 us  [on_device(): pl.pallas_call(functools.partial(step_kernel, wires, lax.axis_size('len')...]
    unnamed x8 -> x0, other arithmetic: 5.72 us -> none
    unnamed x7 -> x22, local copies, waits for them, and re-layouts: 2.81 us -> 8.07 us
    reshape x3 -> x0, local copies, waits for them, and re-layouts: 1.48 us -> none  [the longest x2 1.47 us: unlay(): return x.transpose(1, 0, 2).reshape(1, 1, parts, slots)]
    pad x1 -> x0, local copies, waits for them, and re-layouts: 1.38 us -> none  [on_device(): jnp.pad(nodes.T, ((0, 0), (0, node_pad - node_count)), constant_values=-1)]
    select_n x2 -> x0, other arithmetic: 0.87 us -> none  [the longest x1 0.76 us: on_device(): ghost % block_slots]
    broadcast_in_dim x2 -> x0, local copies, waits for them, and re-layouts: 0.78 us -> none  [on_device(): jnp.repeat(element_stiffness[0, 0], node_pad)]
where the time goes in v1:
time: 51.7 us; the launch traced here: 51.1 us
  Pallas kernels  42.4 us (82%)
  local copies, waits for them, and re-layouts  8.07 us (16%)
  between operations  0.67 us (1%)
    pallas_call x1, Pallas kernels, on_device(): pl.pallas_call(functools.partial(step_kernel, wires, lax.axis_size('len')...  42.4 us
    unnamed x22, local copies, waits for them, and re-layouts  8.07 us

profile of v1, /device:TPU:0, one launch (start us, length us, event | category | flops | bytes accessed | tf_op | source)
XLA Modules:
  0.0 51.1 jit_solution(16046778298875148244)
XLA Ops:
  0.6 0.0 copy-start.7
  0.6 0.0 copy-start.9
  0.7 0.7 %copy-done.7 = s32[1,1,768]{2,1,0:T(1,128)S(1)} copy-done((s32[1,1,768]{2,1,0:T(1,128)S(1)}, s32[1,1,768]{2,1,0:T(1,128)}, u32[]{:S(2)}) %copy-start.7) | copy-done | bytes 3096
  1.3 0.0 copy-done.9
  1.3 0.0 copy-start
  1.3 0.9 %copy-done = f32[375,125]{1,0:T(8,128)S(1)} copy-done((f32[375,125]{1,0:T(8,128)S(1)}, f32[375,125]{1,0:T(8,128)}, u32[]{:S(2)}) %copy-start) | copy-done | bytes 187524
  2.2 0.0 copy-start.1
  2.3 0.8 %copy-done.1 = f32[1,1,3,3584]{3,1,2,0:T(1,128)S(1)} copy-done((f32[1,1,3,3584]{3,1,2,0:T(1,128)S(1)}, f32[1,1,3,3584]{3,1,2,0:T(1,128)}, u32[]{:S(2)}) %copy-start.1) | copy-done | bytes 43032
  3.0 0.0 copy-start.2
  3.0 0.8 %copy-done.2 = f32[1,1,3,3584]{3,1,2,0:T(1,128)S(1)} copy-done((f32[1,1,3,3584]{3,1,2,0:T(1,128)S(1)}, f32[1,1,3,3584]{3,1,2,0:T(1,128)}, u32[]{:S(2)}) %copy-start.2) | copy-done | bytes 43032
  3.8 0.0 copy-start.3
  3.8 0.8 %copy-done.3 = s32[1,1,125,64]{2,3,1,0:T(8,128)S(1)} copy-done((s32[1,1,125,64]{2,3,1,0:T(8,128)S(1)}, s32[1,1,125,64]{2,3,1,0:T(8,128)}, u32[]{:S(2)}) %copy-start.3) | copy-done | bytes 32024
  4.6 0.0 copy-start.4
  4.6 0.8 %copy-done.4 = s32[1,1,4,2048]{3,2,1,0:T(4,128)S(1)} copy-done((s32[1,1,4,2048]{3,2,1,0:T(4,128)S(1)}, s32[1,1,4,2048]{3,2,1,0:T(4,128)}, u32[]{:S(2)}) %copy-start.4) | copy-done | bytes 32792
  5.3 0.0 copy-start.5
  5.3 0.8 %copy-done.5 = s32[1,1,4,2048]{3,2,1,0:T(4,128)S(1)} copy-done((s32[1,1,4,2048]{3,2,1,0:T(4,128)S(1)}, s32[1,1,4,2048]{3,2,1,0:T(4,128)}, u32[]{:S(2)}) %copy-start.5) | copy-done | bytes 32792
  6.1 0.0 copy-start.6
  6.1 0.7 %copy-done.6 = f32[1,1,3584]{2,1,0:T(1,128)S(1)} copy-done((f32[1,1,3584]{2,1,0:T(1,128)S(1)}, f32[1,1,3584]{2,1,0:T(1,128)}, u32[]{:S(2)}) %copy-start.6) | copy-done | bytes 14360
  6.8 0.0 copy-start.8
  6.8 0.7 %copy-done.8 = s32[1,1,768]{2,1,0:T(1,128)S(1)} copy-done((s32[1,1,768]{2,1,0:T(1,128)S(1)}, s32[1,1,768]{2,1,0:T(1,128)}, u32[]{:S(2)}) %copy-start.8) | copy-done | bytes 3096
  7.5 42.4 %steps.1 = (f32[1,3,1,3584]{3,2,1,0:T(1,128)S(1)}, f32[1,3,1,3584]{3,2,1,0:T(1,128)S(1)}) custom-call(f32[1,3,1,3584]{3,2,1,0:T(1,128)S(1)} %bitcast.9, f32[1,3,1,3584]{3,2,1,0:T(1,128)S(1)} %bitcast.10, s32[1,1,64,125]{3,2,1,0:T(8,128)S(1)} %bitcast.13, f32[1,1,64]{2,1,0:T(1,128)S(1)} %copy-done.9, f32[375,125]{1,0:T(8,128)S(1)} %copy-done, ...), custom_call_target="tpu_custom_call" | custom-call | tf_op jit(solution)/shard_map/steps/pallas_call | solution.py:359
  49.9 0.6 %copy.16 = f32[1,1,3,3584]{3,1,2,0:T(1,128)} copy(f32[1,1,3,3584]{3,1,2,0:T(1,128)S(1)} %bitcast.12) | data formatting | bytes 86016
  50.5 0.6 %copy.17 = f32[1,1,3,3584]{3,1,2,0:T(1,128)} copy(f32[1,1,3,3584]{3,1,2,0:T(1,128)S(1)} %bitcast.11) | data formatting | bytes 86016
Async XLA Ops:
  0.6 0.7 %copy-start.7 = (s32[1,1,768]{2,1,0:T(1,128)S(1)}, s32[1,1,768]{2,1,0:T(1,128)}, u32[]{:S(2)}) copy-start(s32[1,1,768]{2,1,0:T(1,128)} %left_in.1) | copy-start | bytes 9220
  0.6 0.7 %copy-start.9 = (f32[1,1,64]{2,1,0:T(1,128)S(1)}, f32[1,1,64]{2,1,0:T(1,128)}, u32[]{:S(2)}) copy-start(f32[1,1,64]{2,1,0:T(1,128)} %stiff_in.1) | copy-start | bytes 772
  1.3 0.9 %copy-start = (f32[375,125]{1,0:T(8,128)S(1)}, f32[375,125]{1,0:T(8,128)}, u32[]{:S(2)}) copy-start(f32[375,125]{1,0:T(8,128)} %grad_in.1) | copy-start | bytes 562504
  2.2 0.8 %copy-start.1 = (f32[1,1,3,3584]{3,1,2,0:T(1,128)S(1)}, f32[1,1,3,3584]{3,1,2,0:T(1,128)}, u32[]{:S(2)}) copy-start(f32[1,1,3,3584]{3,1,2,0:T(1,128)} %param.10) | copy-start | bytes 129028
  3.0 0.8 %copy-start.2 = (f32[1,1,3,3584]{3,1,2,0:T(1,128)S(1)}, f32[1,1,3,3584]{3,1,2,0:T(1,128)}, u32[]{:S(2)}) copy-start(f32[1,1,3,3584]{3,1,2,0:T(1,128)} %param.11) | copy-start | bytes 129028
  3.8 0.8 %copy-start.3 = (s32[1,1,125,64]{2,3,1,0:T(8,128)S(1)}, s32[1,1,125,64]{2,3,1,0:T(8,128)}, u32[]{:S(2)}) copy-start(s32[1,1,125,64]{2,3,1,0:T(8,128)} %param.12) | copy-start | bytes 96004
  4.6 0.8 %copy-start.4 = (s32[1,1,4,2048]{3,2,1,0:T(4,128)S(1)}, s32[1,1,4,2048]{3,2,1,0:T(4,128)}, u32[]{:S(2)}) copy-start(s32[1,1,4,2048]{3,2,1,0:T(4,128)} %slots_in.1) | copy-start | bytes 98308
  5.3 0.8 %copy-start.5 = (s32[1,1,4,2048]{3,2,1,0:T(4,128)S(1)}, s32[1,1,4,2048]{3,2,1,0:T(4,128)}, u32[]{:S(2)}) copy-start(s32[1,1,4,2048]{3,2,1,0:T(4,128)} %live_in.1) | copy-start | bytes 98308
  6.1 0.7 %copy-start.6 = (f32[1,1,3584]{2,1,0:T(1,128)S(1)}, f32[1,1,3584]{2,1,0:T(1,128)}, u32[]{:S(2)}) copy-start(f32[1,1,3584]{2,1,0:T(1,128)} %mass_in.1) | copy-start | bytes 43012
  6.8 0.7 %copy-start.8 = (s32[1,1,768]{2,1,0:T(1,128)S(1)}, s32[1,1,768]{2,1,0:T(1,128)}, u32[]{:S(2)}) copy-start(s32[1,1,768]{2,1,0:T(1,128)} %right_in.1) | copy-start | bytes 9220

commit v2 on v1

--- a/solution.py
+++ b/solution.py
@@ -13,6 +13,10 @@
 block_slots = 224
 block_elements = 4
 LANES = 128
+ARGS = 10
+VMEM_BYTES = 67_043_328
+FIRST = (8, 9, 0)
+LATER = (1, 2, 3, 4, 5, 6, 7)
 BLOCK_SCALE, BLOCK_SHIFT = 4682, 20
 SUB = 8
 f32 = jnp.float32
@@ -36,6 +40,24 @@
     wires,
     segments,
     chunk,
+    *refs,
+):
+    sources, refs = refs[:ARGS], refs[ARGS:]
+    inputs, in_sem, refs = refs[2 : 2 + ARGS], refs[2 + ARGS], refs[:2] + refs[3 + ARGS :]
+    copies = [
+        pltpu.make_async_copy(source, target, in_sem.at[i])
+        for i, (source, target) in enumerate(zip(sources, inputs))
+    ]
+    for i in FIRST + LATER:
+        copies[i].start()
+    run(wires, segments, chunk, copies, *inputs, *refs)
+
+
+def run(
+    wires,
+    segments,
+    chunk,
+    copies,
     u_in, p_in, nodes_in, stiff_in, grad_in, mass_in, left_in, right_in, slots_in, live_in,
     u_out, p_out,
     u_ref, p_ref, mass_ref,
@@ -97,6 +119,8 @@
             here = inside[:, start : start + LANES]
             hot[:, at + start : at + start + LANES] = jnp.where(ids == here, 1.0, 0.0).astype(bf16)
 
+    for i in FIRST:
+        copies[i].wait()
     u_ref[...] = jnp.zeros_like(u_ref)
     p_ref[...] = jnp.zeros_like(p_ref)
     for b in range(blocks):
@@ -104,7 +128,6 @@
         for c in range(parts):
             row = slice(b * SUB + c, b * SUB + c + 1)
             u_ref[row, :block_slots] = u_in[0, c, :, lanes]
-            p_ref[row, :block_slots] = p_in[0, c, :, lanes]
     for d in range(others):
         fill(c_hot, cb_ref, d * pairs, slots_in[0, 0, pl.ds(partner(d), 1), :], live_in[0, 0, pl.ds(partner(d), 1), :])
 
@@ -117,12 +140,16 @@
         g_recv[:, 1] = jnp.zeros((ITERS,) + g_recv.shape[2:], f32)
 
     def prepare():
+        for i in LATER:
+            copies[i].wait()
         row8 = lax.broadcasted_iota(jnp.int32, (SUB, wide), 0)
         lane8 = lax.broadcasted_iota(jnp.int32, (SUB, wide), 1)
         for b in range(blocks):
             at = slice(b * SUB, (b + 1) * SUB)
             lanes = slice(b * block_slots, (b + 1) * block_slots)
             mass_ref[at, :] = jnp.where((row8 == 3) & (lane8 >= block_slots), 1.0, 0.0)
+            for c in range(parts):
+                p_ref[b * SUB + c : b * SUB + c + 1, :block_slots] = p_in[0, c, :, lanes]
             mass_ref[b * SUB + 3 : b * SUB + 4, :block_slots] = mass_in[0, :, lanes]
         fill(g_hot, gb_ref, 0, left_in[0], None)
         fill(g_hot, gb_ref, ghosts, right_in[0], None)
@@ -359,9 +386,11 @@
     results = pl.pallas_call(
         functools.partial(step_kernel, wires, lax.axis_size("len"), 512),
         out_shape=[jax.ShapeDtypeStruct(turned.shape, f32)] * 2,
-        in_specs=[vmem] * len(args),
+        in_specs=[pl.BlockSpec(memory_space=pl.ANY)] * len(args),
         out_specs=[vmem] * 2,
-        scratch_shapes=[
+        scratch_shapes=[pltpu.VMEM(x.shape, x.dtype) for x in args]
+        + [pltpu.SemaphoreType.DMA((len(args),))]
+        + [
             pltpu.VMEM((rows, wide), f32),
             pltpu.VMEM((rows, wide), f32),
             pltpu.VMEM((rows, wide), f32),
@@ -385,7 +414,7 @@
             pltpu.SemaphoreType.DMA((ITERS, 2)),
         ],
         compiler_params=pltpu.CompilerParams(
-            collective_id=0, has_side_effects=True, vmem_limit_bytes=48 * 1024 * 1024
+            collective_id=0, has_side_effects=True, vmem_limit_bytes=VMEM_BYTES
         ),
         name="steps",
     )(*args)

time: 51.7 us -> 46.7 us (0.903)
  local copies, waits for them, and re-layouts: 8.07 us -> 2.04 us
  Pallas kernels: 42.4 us -> 43.9 us
    unnamed x22 -> x4, local copies, waits for them, and re-layouts: 8.07 us -> 2.04 us
    pallas_call x1, Pallas kernels: 42.4 us -> 43.9 us  [on_device(): pl.pallas_call(functools.partial(step_kernel, wires, lax.axis_size('len')...]
where the time goes in v2:
time: 46.7 us; the launch traced here: 46.5 us
  Pallas kernels  43.9 us (94%)
  local copies, waits for them, and re-layouts  2.04 us (4%)
  between operations  0.65 us (1%)
    pallas_call x1, Pallas kernels, on_device(): pl.pallas_call(functools.partial(step_kernel, wires, lax.axis_size('len')...  43.9 us
    unnamed x4, local copies, waits for them, and re-layouts  2.04 us

profile of v2, /device:TPU:0, one launch (start us, length us, event | category | flops | bytes accessed | tf_op | source)
XLA Modules:
  0.0 46.5 jit_solution(6194557404546094236)
XLA Ops:
  0.6 43.9 %steps.1 = (f32[1,3,1,3584]{3,2,1,0:T(1,128)}, f32[1,3,1,3584]{3,2,1,0:T(1,128)}) custom-call(f32[1,3,1,3584]{3,2,1,0:T(1,128)} %bitcast.9, f32[1,3,1,3584]{3,2,1,0:T(1,128)} %bitcast.10, s32[1,1,64,125]{3,2,1,0:T(8,128)} %bitcast.13, f32[1,1,64]{2,1,0:T(1,128)} %refs_3_.1, f32[375,125]{1,0:T(8,128)} %refs_4_.1, f32[1,1,3584]{2,1,0:T(1,128)} %refs_5_.1, ...), custom_call_target="tpu_custom_call" | custom-call | tf_op jit(solution)/shard_map/steps/pallas_call | solution.py:386
  44.5 0.0 copy-start
  44.5 1.4 %copy.16 = f32[1,1,3,3584]{3,1,2,0:T(1,128)} copy(f32[1,1,3,3584]{3,1,2,0:T(1,128)} %bitcast.12) | data formatting | bytes 86016
  45.9 0.0 copy-done
  45.9 0.6 %copy.17 = f32[1,1,3,3584]{3,1,2,0:T(1,128)} copy(f32[1,1,3,3584]{3,1,2,0:T(1,128)S(1)} %bitcast.11) | data formatting | bytes 86016
Async XLA Ops:
  44.5 1.4 %copy-start = (f32[1,3,1,3584]{3,2,1,0:T(1,128)S(1)}, f32[1,3,1,3584]{3,2,1,0:T(1,128)}, u32[]{:S(2)}) copy-start(f32[1,3,1,3584]{3,2,1,0:T(1,128)} %get-tuple-element.5) | copy-start | bytes 129028

commit v3 on v2

--- a/solution.py
+++ b/solution.py
@@ -104,6 +104,12 @@
     def _():
         pl.semaphore_signal(barrier, inc=1, device_id={"len": seg + 1}, device_id_type=MESH)
 
+    def match(slots):
+        ids = lax.broadcasted_iota(jnp.int32, (wide, LANES), 0).astype(bf16)
+        here = jnp.broadcast_to(slots.astype(f32), (2 * SUB, LANES)).astype(bf16)
+        here = jnp.concatenate([here] * (wide // (2 * SUB)), axis=0)
+        return jnp.where(ids == here, jnp.ones((), bf16), jnp.zeros((), bf16))
+
     def block_of(slots):
         return (slots * BLOCK_SCALE) >> BLOCK_SHIFT
 
@@ -115,9 +121,9 @@
             which = jnp.where(live > 0, which, -1)
         base_ref[:, at : at + count] = jnp.broadcast_to(which, (SUB, count))
         for start in range(0, count, LANES):
-            ids = lax.broadcasted_iota(jnp.int32, (wide, LANES), 0)
             here = inside[:, start : start + LANES]
-            hot[:, at + start : at + start + LANES] = jnp.where(ids == here, 1.0, 0.0).astype(bf16)
+            group, lane = divmod(at + start, hot.shape[2])
+            hot[group, :, lane : lane + LANES] = match(here)
 
     for i in FIRST:
         copies[i].wait()
@@ -169,9 +175,7 @@
         for b in range(blocks):
             for e in range(block_elements):
                 one = b * block_elements + e
-                ids = lax.broadcasted_iota(jnp.int32, (wide, node_pad), 0)
-                hot = jnp.where(ids == nodes_ref[one : one + 1, :], 1.0, 0.0).astype(bf16)
-                e_hot[b, :, e * node_pad : (e + 1) * node_pad] = hot
+                e_hot[b, :, e * node_pad : (e + 1) * node_pad] = match(nodes_ref[one : one + 1, :])
 
     last = segments - 1
     pl.semaphore_wait(
@@ -190,7 +194,7 @@
 
     def take(packed, hot, base_ref, start, width):
         cols = slice(start, start + width)
-        picked = dot(packed, hot[:, cols])
+        picked = dot(packed, hot[start // width])
         which = base_ref[:, cols]
         total = jnp.zeros((SUB, width), f32)
         for b in range(blocks):
@@ -203,11 +207,11 @@
         values = jnp.where(rows_of(width) < 4, high, values - high)
         which = base_ref[:, cols]
         spread = jnp.concatenate([jnp.where(which == b, values, 0.0) for b in range(blocks)], axis=0)
-        return dot_nt(spread.astype(bf16), hot[:, cols])
+        return dot_nt(spread.astype(bf16), hot[start // width])
 
     def take_list(packed, hot, base_ref, start, count, out_ref):
         half = count // 2
-        width = chunk if half % chunk == 0 else half
+        width = hot.shape[2]
         for at in range(0, half, width):
             first = take(packed, hot, base_ref, start + at, width)
             second = take(packed, hot, base_ref, start + half + at, width)
@@ -215,7 +219,7 @@
 
     def put_list(values, hot, base_ref, start, count, total):
         half = count // 2
-        width = chunk if half % chunk == 0 else half
+        width = hot.shape[2]
         for at in range(0, half, width):
             here = values[:, at : at + width]
             turned = pltpu.roll(here, 4, 0)
@@ -377,6 +381,7 @@
     rows = blocks * SUB
     pairs = contact_slots.shape[3]
     ghosts = left_ghost.shape[2]
+    c_width, g_width = (512 if x % 512 == 0 else x for x in (pairs // 2, ghosts // 2))
     assert blocks % 2 == 0 and elements <= LANES and node_pad == LANES
     assert all((x * BLOCK_SCALE) >> BLOCK_SHIFT == x // block_slots for x in range(blocks * block_slots))
 
@@ -394,8 +399,8 @@
             pltpu.VMEM((rows, wide), f32),
             pltpu.VMEM((rows, wide), f32),
             pltpu.VMEM((rows, wide), f32),
-            pltpu.VMEM((wide, others * pairs), bf16),
-            pltpu.VMEM((wide, 2 * ghosts), bf16),
+            pltpu.VMEM((others * pairs // c_width, wide, c_width), bf16),
+            pltpu.VMEM((2 * ghosts // g_width, wide, g_width), bf16),
             pltpu.VMEM((blocks, wide, block_elements * node_pad), bf16),
             pltpu.VMEM((SUB, others * pairs), jnp.int32),
             pltpu.VMEM((SUB, 2 * ghosts), jnp.int32),

time: 46.7 us -> 44.8 us (0.959)
  Pallas kernels: 43.9 us -> 42 us
    pallas_call x1, Pallas kernels: 43.9 us -> 42 us  [on_device(): pl.pallas_call(functools.partial(step_kernel, wires, lax.axis_size('len')...]
where the time goes in v3:
time: 44.8 us; the launch traced here: 44.6 us
  Pallas kernels  42 us (94%)
  local copies, waits for them, and re-layouts  2.04 us (5%)
  between operations  0.65 us (1%)
    pallas_call x1, Pallas kernels, on_device(): pl.pallas_call(functools.partial(step_kernel, wires, lax.axis_size('len')...  42 us
    unnamed x4, local copies, waits for them, and re-layouts  2.04 us

profile of v3, /device:TPU:0, one launch (start us, length us, event | category | flops | bytes accessed | tf_op | source)
XLA Modules:
  0.0 44.6 jit_solution(15891558745769143846)
XLA Ops:
  0.6 42.0 %steps.1 = (f32[1,3,1,3584]{3,2,1,0:T(1,128)}, f32[1,3,1,3584]{3,2,1,0:T(1,128)}) custom-call(f32[1,3,1,3584]{3,2,1,0:T(1,128)} %bitcast.9, f32[1,3,1,3584]{3,2,1,0:T(1,128)} %bitcast.10, s32[1,1,64,125]{3,2,1,0:T(8,128)} %bitcast.13, f32[1,1,64]{2,1,0:T(1,128)} %refs_3_.1, f32[375,125]{1,0:T(8,128)} %refs_4_.1, f32[1,1,3584]{2,1,0:T(1,128)} %refs_5_.1, ...), custom_call_target="tpu_custom_call" | custom-call | tf_op jit(solution)/shard_map/steps/pallas_call | solution.py:391
  42.6 0.0 copy-start
  42.6 1.4 %copy.16 = f32[1,1,3,3584]{3,1,2,0:T(1,128)} copy(f32[1,1,3,3584]{3,1,2,0:T(1,128)} %bitcast.12) | data formatting | bytes 86016
  44.0 0.0 copy-done
  44.0 0.6 %copy.17 = f32[1,1,3,3584]{3,1,2,0:T(1,128)} copy(f32[1,1,3,3584]{3,1,2,0:T(1,128)S(1)} %bitcast.11) | data formatting | bytes 86016
Async XLA Ops:
  42.6 1.4 %copy-start = (f32[1,3,1,3584]{3,2,1,0:T(1,128)S(1)}, f32[1,3,1,3584]{3,2,1,0:T(1,128)}, u32[]{:S(2)}) copy-start(f32[1,3,1,3584]{3,2,1,0:T(1,128)} %get-tuple-element.5) | copy-start | bytes 129028
